TPU v7x, 256 devices: a whole 4x4x8 slice. The times are simulated.
256 devices in a mesh: ctx: 16 (over z, core), row: 4 (over y), col: 4 (over x).
Axes of the slice: x: 4, y: 4, z: 8, core: 2. Of those that a mesh axis runs over, the one named last changes fastest.
Arguments:
- output_grad: bfloat16 [8192, 8192], P('ctx', ('row', 'col')), may hold values from -6 to 6
- conv_out: bfloat16 [8192, 8192], P('ctx', ('row', 'col')), may hold values from -9 to 9
- input_mix: bfloat16 [8192, 4, 256], P('ctx'), may hold values from -0.15625 to 0.15625
- output_mix: bfloat16 [8192, 4, 256], P('ctx'), may hold values from -1 to 1
- step_size: float32 [128, 8192], P(('row', 'col'), 'ctx'), may hold values from 0.5 to 2
- log_decay: float32 [128, 8192], P(('row', 'col'), 'ctx'), may hold values from -2.1 to 0, as said below
- skip_gain: float32 [128], P(('row', 'col')), may hold values from 0.5 to 2
- conv_weight: float32 [4, 8192], P(None, ('row', 'col')), may hold values from -3 to 3
- later_grad: float32 [128, 64, 256], P(('row', 'col')), may hold values from -32 to 32
- proj_weight: bfloat16 [8192, 8192], P('col', 'row'), may hold values from -0.0625 to 0.0625
Outputs:
- hidden_grad: bfloat16 [8192, 8192], P('ctx', ('col', 'row'))
- x_grad: bfloat16 [8192, 8192], P('ctx', ('row', 'col'))
- state_grad: float32 [16, 128, 64, 256], P('ctx', ('row', 'col'))
Inputs may be any that keep to these rules, and one draw needn't show every extreme that they name: `log_decay`: the forward pass's log decay of each head at each token.
All inputs are finite; a program needn't handle non-finite values.
Results may differ from a plain program's by a relative error of at most 0.022.
Values may be sent and summed in bfloat16 or wider, within the bound.
No kernel may reach another device: no remote copies, remote signals or barrier semaphores. Data moves between devices by JAX's collectives and lax.ppermute only.
A program may use at most 128 MiB of HBM per device.

v0:
```python
import jax
import jax.numpy as jnp
from jax import lax
from jax.sharding import PartitionSpec as P

HD = 64
HPG = 32
KW = 4


def from_behind(value, axis, steps):
    count = lax.axis_size(axis)
    first, last = (max(0, -steps), min(count, count - steps))
    return lax.ppermute(value, axis, [(source, source + steps) for source in range(first, last)])


def on_device(
    output_grad,
    conv_out,
    input_mix,
    output_mix,
    step_size,
    log_decay,
    skip_gain,
    conv_weight,
    later_grad,
    proj_weight,
):
    tokens_dev = output_grad.shape[0]
    heads_dev = step_size.shape[0]
    head_block = lax.axis_index("row") * lax.axis_size("col") + lax.axis_index("col")
    group = head_block * heads_dev // HPG
    write_rows = lax.dynamic_index_in_dim(input_mix, group, 1, keepdims=False)
    read_rows = lax.dynamic_index_in_dim(output_mix, group, 1, keepdims=False)
    cumulative = jnp.cumsum(log_decay, axis=1)
    block_end = cumulative[:, -1]
    decays = jnp.exp(block_end)
    per_head = output_grad.reshape(tokens_dev, heads_dev, HD)
    weighted = (jnp.exp(cumulative).T[:, :, None] * per_head.astype(jnp.float32)).astype(
        jnp.bfloat16
    )
    block_sum = jnp.einsum("shd,sn->hdn", weighted, read_rows, preferred_element_type=jnp.float32)
    is_last = lax.axis_index("ctx") == lax.axis_size("ctx") - 1

    def chain_turn(turn_index, estimate):
        passed = from_behind(
            (block_sum + decays[:, None, None] * estimate).astype(jnp.bfloat16), "ctx", -1
        ).astype(jnp.float32)
        return jnp.where(is_last, later_grad, passed)

    carried = lax.fori_loop(
        0,
        lax.axis_size("ctx") - 1,
        chain_turn,
        jnp.where(is_last, later_grad, jnp.zeros_like(later_grad)),
    )
    state_start = block_sum + decays[:, None, None] * carried
    scores = jnp.dot(write_rows, read_rows.T, preferred_element_type=jnp.float32)
    positions = jnp.arange(tokens_dev)
    causal = positions[None, :] >= positions[:, None]
    offsets = cumulative[:, None, :] - cumulative[:, :, None]
    mixing = (jnp.exp(jnp.where(causal[None], offsets, -jnp.inf)) * scores[None]).astype(
        jnp.bfloat16
    )
    intra = jnp.einsum("hts,shd->thd", mixing, per_head, preferred_element_type=jnp.float32)
    inter = jnp.einsum(
        "hdn,tn->thd", carried, write_rows.astype(jnp.float32), precision=lax.Precision.HIGHEST
    )
    inter = inter * jnp.exp(block_end[:, None] - cumulative).T[:, :, None]
    input_grad = step_size.T[:, :, None] * (intra + inter) + skip_gain[
        None, :, None
    ] * per_head.astype(jnp.float32)
    flat_grad = input_grad.reshape(tokens_dev, heads_dev * HD)
    activated = conv_out.astype(jnp.float32)
    sigma = jax.nn.sigmoid(activated)
    pre_grad = (flat_grad * sigma * (1.0 + activated * (1.0 - sigma))).astype(jnp.bfloat16)
    rim_rows = from_behind(pre_grad[: KW - 1], "ctx", -1)
    extended = jnp.concatenate([pre_grad, rim_rows], axis=0).astype(jnp.float32)
    accum = jnp.zeros(pre_grad.shape, jnp.float32)
    for tap in range(KW):
        accum = accum + conv_weight[tap][None, :] * extended[tap : tap + tokens_dev]
    x_grad = accum.astype(jnp.bfloat16)
    partial_grad = lax.dot_general(
        lax.all_gather(x_grad, "col", axis=1, tiled=True),
        proj_weight,
        (((1,), (1,)), ((), ())),
        preferred_element_type=jnp.float32,
    )
    hidden_grad = lax.psum_scatter(
        partial_grad.astype(jnp.bfloat16), "row", scatter_dimension=1, tiled=True
    )
    return (hidden_grad, x_grad, state_start[None])


def solution(mesh):
    return jax.shard_map(
        on_device,
        mesh=mesh,
        in_specs=(
            P("ctx", ("row", "col")),
            P("ctx", ("row", "col")),
            P("ctx", None, None),
            P("ctx", None, None),
            P(("row", "col"), "ctx"),
            P(("row", "col"), "ctx"),
            P(("row", "col")),
            P(None, ("row", "col")),
            P(("row", "col"), None, None),
            P("col", "row"),
        ),
        out_specs=(
            P("ctx", ("col", "row")),
            P("ctx", ("row", "col")),
            P("ctx", ("row", "col"), None, None),
        ),
        check_vma=False,
    )
```

profile of v0, /device:TPU:1, one launch (start us, length us, event | category | flops | bytes accessed | tf_op | source)
XLA Modules:
  0.0 251.9 jit_solution(11634387616972478772)
XLA Ops:
  7.2 2.3 reduce-window.6
  9.5 0.2 slice_reduce_fusion
  9.8 0.2 slice_reduce_fusion.1
  10.1 1.3 copy.26
  11.5 2.6 %constant_dynamic-slice_fusion = (bf16[512,1,256]{2,1,0:T(2,128)(2,1)S(1)}, bf16[512,1,256]{2,1,0:T(2,128)(2,1)S(1)}) fusion(bf16[512,4,256]{2,1,0:T(4,128)(2,1)} %param.15, s32[]{:T(128)S(6)} %select_n.30, bf16[512,4,256]{2,1,0:T(4,128)(2,1)} %param.14), kind=kLoop, calls=%fused_computation.48 | loop fusion | bytes 1048580 | tf_op jit(solution)/shard_map/jit(dynamic_index_in_dim)/dynamic_slice | solution.py:34
  14.1 0.3 fusion.17
  14.5 1.3 fusion.20
  15.8 4.3 %fusion.2 = f32[512,8,64]{0,2,1:T(8,128)} fusion(bf16[512,8,64]{0,2,1:T(8,128)(2,1)S(1)} %bitcast.41, f32[512,512]{1,0:T(8,128)} %fusion.20, f32[8,512]{1,0:T(8,128)S(1)} %get-tuple-element.49, pred[512,512]{1,0:T(8,128)(4,1)S(1)} %iota_compare_fusion), kind=kOutput, calls=%fused_computation.6 | convolution fusion | flops 276824064 | bytes 2899968 | tf_op jit(solution)/shard_map/hts,shd->thd/dot_general | solution.py:65
  20.1 119.6 %while.10 = (s32[]{:T(128)}, f32[8,64,256]{2,1,0:T(8,128)S(1)}, pred[]{:T(512)}, f32[8]{0:T(128)S(1)}, f32[8,64,256]{2,1,0:T(8,128)S(1)}, /*index=5*/f32[8,64,256]{2,1,0:T(8,128)S(1)}, s32[]{:T(128)}) while((s32[]{:T(128)}, f32[8,64,256]{2,1,0:T(8,128)S(1)}, pred[]{:T(512)}, f32[8]{0:T(128)S(1)}, f32[8,64,256]{2,1,0:T(8,128)S(1)}, ...), condition=%wide.region_3.4_spmd, body=%wide.region_2.3_spmd.sunk | while | flops 655362 | bytes 3670166 | solution.py:51
  20.2 5.2 %collective-permute-start = (bf16[8,64,256]{2,1,0:T(8,128)(2,1)S(1)}, bf16[8,64,256]{2,1,0:T(8,128)(2,1)S(1)}, u32[]{:S(2)}, u32[]{:S(2)}) collective-permute-start(bf16[8,64,256]{2,1,0:T(8,128)(2,1)S(1)} %add_convert_fusion.2), channel_id=1, source_target_pairs={{16,0},{32,16},{48,32},{64,48},{80,64},{96,80},{112,96},{128,112},... | collective-permute-start | bytes 786440 | tf_op jit(solution)/shard_map/while/body/eval_jaxpr/ppermute | solution.py:14
  25.4 3.8 %collective-permute-done = bf16[8,64,256]{2,1,0:T(8,128)(2,1)S(1)} collective-permute-done((bf16[8,64,256]{2,1,0:T(8,128)(2,1)S(1)}, bf16[8,64,256]{2,1,0:T(8,128)(2,1)S(1)}, u32[]{:S(2)}, u32[]{:S(2)}) %collective-permute-start) | collective-permute-done | bytes 262176 | tf_op jit(solution)/shard_map/while/body/eval_jaxpr/ppermute | solution.py:14
  29.3 0.1 add_convert_fusion.2
  29.4 1.9 collective-permute-start
  31.3 5.8 %collective-permute-done = bf16[8,64,256]{2,1,0:T(8,128)(2,1)S(1)} collective-permute-done((bf16[8,64,256]{2,1,0:T(8,128)(2,1)S(1)}, bf16[8,64,256]{2,1,0:T(8,128)(2,1)S(1)}, u32[]{:S(2)}, u32[]{:S(2)}) %collective-permute-start) | collective-permute-done | bytes 262176 | tf_op jit(solution)/shard_map/while/body/eval_jaxpr/ppermute | solution.py:14
  37.2 0.1 add_convert_fusion.2
  37.3 1.9 collective-permute-start
  39.2 5.8 %collective-permute-done = bf16[8,64,256]{2,1,0:T(8,128)(2,1)S(1)} collective-permute-done((bf16[8,64,256]{2,1,0:T(8,128)(2,1)S(1)}, bf16[8,64,256]{2,1,0:T(8,128)(2,1)S(1)}, u32[]{:S(2)}, u32[]{:S(2)}) %collective-permute-start) | collective-permute-done | bytes 262176 | tf_op jit(solution)/shard_map/while/body/eval_jaxpr/ppermute | solution.py:14
  45.0 0.1 add_convert_fusion.2
  45.2 1.9 collective-permute-start
  47.1 5.8 %collective-permute-done = bf16[8,64,256]{2,1,0:T(8,128)(2,1)S(1)} collective-permute-done((bf16[8,64,256]{2,1,0:T(8,128)(2,1)S(1)}, bf16[8,64,256]{2,1,0:T(8,128)(2,1)S(1)}, u32[]{:S(2)}, u32[]{:S(2)}) %collective-permute-start) | collective-permute-done | bytes 262176 | tf_op jit(solution)/shard_map/while/body/eval_jaxpr/ppermute | solution.py:14
  52.9 0.1 add_convert_fusion.2
  53.1 1.9 collective-permute-start
  55.0 5.8 %collective-permute-done = bf16[8,64,256]{2,1,0:T(8,128)(2,1)S(1)} collective-permute-done((bf16[8,64,256]{2,1,0:T(8,128)(2,1)S(1)}, bf16[8,64,256]{2,1,0:T(8,128)(2,1)S(1)}, u32[]{:S(2)}, u32[]{:S(2)}) %collective-permute-start) | collective-permute-done | bytes 262176 | tf_op jit(solution)/shard_map/while/body/eval_jaxpr/ppermute | solution.py:14
  60.8 0.1 add_convert_fusion.2
  60.9 1.9 collective-permute-start
  62.9 5.8 %collective-permute-done = bf16[8,64,256]{2,1,0:T(8,128)(2,1)S(1)} collective-permute-done((bf16[8,64,256]{2,1,0:T(8,128)(2,1)S(1)}, bf16[8,64,256]{2,1,0:T(8,128)(2,1)S(1)}, u32[]{:S(2)}, u32[]{:S(2)}) %collective-permute-start) | collective-permute-done | bytes 262176 | tf_op jit(solution)/shard_map/while/body/eval_jaxpr/ppermute | solution.py:14
  68.7 0.1 add_convert_fusion.2
  68.8 1.9 collective-permute-start
  70.8 5.8 %collective-permute-done = bf16[8,64,256]{2,1,0:T(8,128)(2,1)S(1)} collective-permute-done((bf16[8,64,256]{2,1,0:T(8,128)(2,1)S(1)}, bf16[8,64,256]{2,1,0:T(8,128)(2,1)S(1)}, u32[]{:S(2)}, u32[]{:S(2)}) %collective-permute-start) | collective-permute-done | bytes 262176 | tf_op jit(solution)/shard_map/while/body/eval_jaxpr/ppermute | solution.py:14
  76.6 0.1 add_convert_fusion.2
  76.7 1.9 collective-permute-start
  78.6 5.8 %collective-permute-done = bf16[8,64,256]{2,1,0:T(8,128)(2,1)S(1)} collective-permute-done((bf16[8,64,256]{2,1,0:T(8,128)(2,1)S(1)}, bf16[8,64,256]{2,1,0:T(8,128)(2,1)S(1)}, u32[]{:S(2)}, u32[]{:S(2)}) %collective-permute-start) | collective-permute-done | bytes 262176 | tf_op jit(solution)/shard_map/while/body/eval_jaxpr/ppermute | solution.py:14
  84.5 0.1 add_convert_fusion.2
  84.6 1.9 collective-permute-start
  86.5 5.8 %collective-permute-done = bf16[8,64,256]{2,1,0:T(8,128)(2,1)S(1)} collective-permute-done((bf16[8,64,256]{2,1,0:T(8,128)(2,1)S(1)}, bf16[8,64,256]{2,1,0:T(8,128)(2,1)S(1)}, u32[]{:S(2)}, u32[]{:S(2)}) %collective-permute-start) | collective-permute-done | bytes 262176 | tf_op jit(solution)/shard_map/while/body/eval_jaxpr/ppermute | solution.py:14
  92.4 0.1 add_convert_fusion.2
  92.5 1.9 collective-permute-start
  94.4 5.8 %collective-permute-done = bf16[8,64,256]{2,1,0:T(8,128)(2,1)S(1)} collective-permute-done((bf16[8,64,256]{2,1,0:T(8,128)(2,1)S(1)}, bf16[8,64,256]{2,1,0:T(8,128)(2,1)S(1)}, u32[]{:S(2)}, u32[]{:S(2)}) %collective-permute-start) | collective-permute-done | bytes 262176 | tf_op jit(solution)/shard_map/while/body/eval_jaxpr/ppermute | solution.py:14
  100.3 0.1 add_convert_fusion.2
  100.4 1.9 collective-permute-start
  102.3 5.8 %collective-permute-done = bf16[8,64,256]{2,1,0:T(8,128)(2,1)S(1)} collective-permute-done((bf16[8,64,256]{2,1,0:T(8,128)(2,1)S(1)}, bf16[8,64,256]{2,1,0:T(8,128)(2,1)S(1)}, u32[]{:S(2)}, u32[]{:S(2)}) %collective-permute-start) | collective-permute-done | bytes 262176 | tf_op jit(solution)/shard_map/while/body/eval_jaxpr/ppermute | solution.py:14
  108.1 0.1 add_convert_fusion.2
  108.3 1.9 collective-permute-start
  110.2 5.8 %collective-permute-done = bf16[8,64,256]{2,1,0:T(8,128)(2,1)S(1)} collective-permute-done((bf16[8,64,256]{2,1,0:T(8,128)(2,1)S(1)}, bf16[8,64,256]{2,1,0:T(8,128)(2,1)S(1)}, u32[]{:S(2)}, u32[]{:S(2)}) %collective-permute-start) | collective-permute-done | bytes 262176 | tf_op jit(solution)/shard_map/while/body/eval_jaxpr/ppermute | solution.py:14
  116.0 0.1 add_convert_fusion.2
  116.2 1.9 collective-permute-start
  118.1 5.8 %collective-permute-done = bf16[8,64,256]{2,1,0:T(8,128)(2,1)S(1)} collective-permute-done((bf16[8,64,256]{2,1,0:T(8,128)(2,1)S(1)}, bf16[8,64,256]{2,1,0:T(8,128)(2,1)S(1)}, u32[]{:S(2)}, u32[]{:S(2)}) %collective-permute-start) | collective-permute-done | bytes 262176 | tf_op jit(solution)/shard_map/while/body/eval_jaxpr/ppermute | solution.py:14
  123.9 0.1 add_convert_fusion.2
  124.0 1.9 collective-permute-start
  126.0 5.8 %collective-permute-done = bf16[8,64,256]{2,1,0:T(8,128)(2,1)S(1)} collective-permute-done((bf16[8,64,256]{2,1,0:T(8,128)(2,1)S(1)}, bf16[8,64,256]{2,1,0:T(8,128)(2,1)S(1)}, u32[]{:S(2)}, u32[]{:S(2)}) %collective-permute-start) | collective-permute-done | bytes 262176 | tf_op jit(solution)/shard_map/while/body/eval_jaxpr/ppermute | solution.py:14
  131.8 0.1 add_convert_fusion.2
  131.9 1.9 collective-permute-start
  133.9 5.8 %collective-permute-done = bf16[8,64,256]{2,1,0:T(8,128)(2,1)S(1)} collective-permute-done((bf16[8,64,256]{2,1,0:T(8,128)(2,1)S(1)}, bf16[8,64,256]{2,1,0:T(8,128)(2,1)S(1)}, u32[]{:S(2)}, u32[]{:S(2)}) %collective-permute-start) | collective-permute-done | bytes 262176 | tf_op jit(solution)/shard_map/while/body/eval_jaxpr/ppermute | solution.py:14
  139.7 2.0 fusion.5
  141.7 0.3 copy.28
  142.0 1.4 fusion.11
  143.5 1.9 collective-permute-start.1
  145.5 3.0 %collective-permute-done.1 = bf16[3,512]{1,0:T(4,128)(2,1)S(1)} collective-permute-done((bf16[3,512]{1,0:T(4,128)(2,1)S(1)}, bf16[3,512]{1,0:T(4,128)(2,1)S(1)}, u32[]{:S(2)}, u32[]{:S(2)}) %collective-permute-start.1) | collective-permute-done | bytes 3104 | tf_op jit(solution)/shard_map/ppermute | solution.py:14
  148.4 0.1 maximum_convert_fusion
  148.6 1.3 fusion.13
  149.9 52.7 %all-gather.2.cloned.1.call-done = bf16[512,2048]{1,0:T(8,128)(2,1)} async-done(((bf16[512,512]{1,0:T(8,128)(2,1)}), bf16[512,2048]{1,0:T(8,128)(2,1)}) %all-gather.2.cloned.1.call-update) | async-done | bytes 2097168 | tf_op jit(solution)/shard_map/all_gather | solution.py:84
  202.6 9.9 %convolution_convert_fusion = bf16[512,2048]{1,0:T(8,128)(2,1)} fusion(bf16[512,2048]{1,0:T(8,128)(2,1)} %all-gather.2.cloned.1.call-done, bf16[2048,2048]{1,0:T(8,128)(2,1)} %param.21), kind=kOutput, calls=%fused_computation.5 | convolution fusion | flops 4296015872 | bytes 12582912 | tf_op jit(solution)/shard_map/dot_general | solution.py:83
  212.5 0.9 add_bitcast_fusion
  213.4 31.6 %reduce-scatter.2.cloned.1.call-done = bf16[512,512]{1,0:T(8,128)(2,1)} async-done(((bf16[512,2048]{1,0:T(8,128)(2,1)}), bf16[512,512]{1,0:T(8,128)(2,1)}) %reduce-scatter.2.cloned.1.call-update) | async-done | bytes 524304 | tf_op jit(solution)/shard_map/reduce_scatter | solution.py:89
  (38 shorter events, 1.5 us)
Async XLA Ops:
  7.2 8.6 %copy-start = (f32[8,64,256]{2,1,0:T(8,128)S(1)}, f32[8,64,256]{2,1,0:T(8,128)}, u32[]{:S(2)}) copy-start(f32[8,64,256]{2,1,0:T(8,128)} %param.20) | copy-start | bytes 1572868
  7.2 195.4 %all-gather.2.cloned.1.call-start = ((), (), s32[]{:S(2)}) async-start(), calls=%async_computation.1 | async-start | bytes 2621440 | tf_op jit(solution)/shard_map/all_gather | solution.py:84
  20.1 119.6 %copy-start.1 = (f32[8,512]{1,0:T(8,128)S(1)}, f32[8,512]{1,0:T(8,128)}, u32[]{:S(2)}) copy-start(f32[8,512]{1,0:T(8,128)} %param.16) | copy-start | bytes 49156
  20.1 119.6 %copy-start.3 = (f32[8]{0:T(128)S(1)}, f32[8]{0:T(128)}, u32[]{:S(2)}) copy-start(f32[8]{0:T(128)} %param.18) | copy-start | bytes 100
  20.2 9.0 %collective-permute-start = (bf16[8,64,256]{2,1,0:T(8,128)(2,1)S(1)}, bf16[8,64,256]{2,1,0:T(8,128)(2,1)S(1)}, u32[]{:S(2)}, u32[]{:S(2)}) collective-permute-start(bf16[8,64,256]{2,1,0:T(8,128)(2,1)S(1)} %add_convert_fusion.2), channel_id=1, source_target_pairs={{16,0},{32,16},{48,32},{64,48},{80,64},{96,80},{112,96},{128,112},... | collective-permute-start | bytes 786440 | tf_op jit(solution)/shard_map/while/body/eval_jaxpr/ppermute | solution.py:14
  29.4 7.7 %collective-permute-start = (bf16[8,64,256]{2,1,0:T(8,128)(2,1)S(1)}, bf16[8,64,256]{2,1,0:T(8,128)(2,1)S(1)}, u32[]{:S(2)}, u32[]{:S(2)}) collective-permute-start(bf16[8,64,256]{2,1,0:T(8,128)(2,1)S(1)} %add_convert_fusion.2), channel_id=1, source_target_pairs={{16,0},{32,16},{48,32},{64,48},{80,64},{96,80},{112,96},{128,112},... | collective-permute-start | bytes 786440 | tf_op jit(solution)/shard_map/while/body/eval_jaxpr/ppermute | solution.py:14
  37.3 7.7 %collective-permute-start = (bf16[8,64,256]{2,1,0:T(8,128)(2,1)S(1)}, bf16[8,64,256]{2,1,0:T(8,128)(2,1)S(1)}, u32[]{:S(2)}, u32[]{:S(2)}) collective-permute-start(bf16[8,64,256]{2,1,0:T(8,128)(2,1)S(1)} %add_convert_fusion.2), channel_id=1, source_target_pairs={{16,0},{32,16},{48,32},{64,48},{80,64},{96,80},{112,96},{128,112},... | collective-permute-start | bytes 786440 | tf_op jit(solution)/shard_map/while/body/eval_jaxpr/ppermute | solution.py:14
  45.2 7.7 %collective-permute-start = (bf16[8,64,256]{2,1,0:T(8,128)(2,1)S(1)}, bf16[8,64,256]{2,1,0:T(8,128)(2,1)S(1)}, u32[]{:S(2)}, u32[]{:S(2)}) collective-permute-start(bf16[8,64,256]{2,1,0:T(8,128)(2,1)S(1)} %add_convert_fusion.2), channel_id=1, source_target_pairs={{16,0},{32,16},{48,32},{64,48},{80,64},{96,80},{112,96},{128,112},... | collective-permute-start | bytes 786440 | tf_op jit(solution)/shard_map/while/body/eval_jaxpr/ppermute | solution.py:14
  53.1 7.7 %collective-permute-start = (bf16[8,64,256]{2,1,0:T(8,128)(2,1)S(1)}, bf16[8,64,256]{2,1,0:T(8,128)(2,1)S(1)}, u32[]{:S(2)}, u32[]{:S(2)}) collective-permute-start(bf16[8,64,256]{2,1,0:T(8,128)(2,1)S(1)} %add_convert_fusion.2), channel_id=1, source_target_pairs={{16,0},{32,16},{48,32},{64,48},{80,64},{96,80},{112,96},{128,112},... | collective-permute-start | bytes 786440 | tf_op jit(solution)/shard_map/while/body/eval_jaxpr/ppermute | solution.py:14
  60.9 7.7 %collective-permute-start = (bf16[8,64,256]{2,1,0:T(8,128)(2,1)S(1)}, bf16[8,64,256]{2,1,0:T(8,128)(2,1)S(1)}, u32[]{:S(2)}, u32[]{:S(2)}) collective-permute-start(bf16[8,64,256]{2,1,0:T(8,128)(2,1)S(1)} %add_convert_fusion.2), channel_id=1, source_target_pairs={{16,0},{32,16},{48,32},{64,48},{80,64},{96,80},{112,96},{128,112},... | collective-permute-start | bytes 786440 | tf_op jit(solution)/shard_map/while/body/eval_jaxpr/ppermute | solution.py:14
  68.8 7.7 %collective-permute-start = (bf16[8,64,256]{2,1,0:T(8,128)(2,1)S(1)}, bf16[8,64,256]{2,1,0:T(8,128)(2,1)S(1)}, u32[]{:S(2)}, u32[]{:S(2)}) collective-permute-start(bf16[8,64,256]{2,1,0:T(8,128)(2,1)S(1)} %add_convert_fusion.2), channel_id=1, source_target_pairs={{16,0},{32,16},{48,32},{64,48},{80,64},{96,80},{112,96},{128,112},... | collective-permute-start | bytes 786440 | tf_op jit(solution)/shard_map/while/body/eval_jaxpr/ppermute | solution.py:14
  76.7 7.7 %collective-permute-start = (bf16[8,64,256]{2,1,0:T(8,128)(2,1)S(1)}, bf16[8,64,256]{2,1,0:T(8,128)(2,1)S(1)}, u32[]{:S(2)}, u32[]{:S(2)}) collective-permute-start(bf16[8,64,256]{2,1,0:T(8,128)(2,1)S(1)} %add_convert_fusion.2), channel_id=1, source_target_pairs={{16,0},{32,16},{48,32},{64,48},{80,64},{96,80},{112,96},{128,112},... | collective-permute-start | bytes 786440 | tf_op jit(solution)/shard_map/while/body/eval_jaxpr/ppermute | solution.py:14
  84.6 7.7 %collective-permute-start = (bf16[8,64,256]{2,1,0:T(8,128)(2,1)S(1)}, bf16[8,64,256]{2,1,0:T(8,128)(2,1)S(1)}, u32[]{:S(2)}, u32[]{:S(2)}) collective-permute-start(bf16[8,64,256]{2,1,0:T(8,128)(2,1)S(1)} %add_convert_fusion.2), channel_id=1, source_target_pairs={{16,0},{32,16},{48,32},{64,48},{80,64},{96,80},{112,96},{128,112},... | collective-permute-start | bytes 786440 | tf_op jit(solution)/shard_map/while/body/eval_jaxpr/ppermute | solution.py:14
  92.5 7.7 %collective-permute-start = (bf16[8,64,256]{2,1,0:T(8,128)(2,1)S(1)}, bf16[8,64,256]{2,1,0:T(8,128)(2,1)S(1)}, u32[]{:S(2)}, u32[]{:S(2)}) collective-permute-start(bf16[8,64,256]{2,1,0:T(8,128)(2,1)S(1)} %add_convert_fusion.2), channel_id=1, source_target_pairs={{16,0},{32,16},{48,32},{64,48},{80,64},{96,80},{112,96},{128,112},... | collective-permute-start | bytes 786440 | tf_op jit(solution)/shard_map/while/body/eval_jaxpr/ppermute | solution.py:14
  100.4 7.7 %collective-permute-start = (bf16[8,64,256]{2,1,0:T(8,128)(2,1)S(1)}, bf16[8,64,256]{2,1,0:T(8,128)(2,1)S(1)}, u32[]{:S(2)}, u32[]{:S(2)}) collective-permute-start(bf16[8,64,256]{2,1,0:T(8,128)(2,1)S(1)} %add_convert_fusion.2), channel_id=1, source_target_pairs={{16,0},{32,16},{48,32},{64,48},{80,64},{96,80},{112,96},{128,112},... | collective-permute-start | bytes 786440 | tf_op jit(solution)/shard_map/while/body/eval_jaxpr/ppermute | solution.py:14
  108.3 7.7 %collective-permute-start = (bf16[8,64,256]{2,1,0:T(8,128)(2,1)S(1)}, bf16[8,64,256]{2,1,0:T(8,128)(2,1)S(1)}, u32[]{:S(2)}, u32[]{:S(2)}) collective-permute-start(bf16[8,64,256]{2,1,0:T(8,128)(2,1)S(1)} %add_convert_fusion.2), channel_id=1, source_target_pairs={{16,0},{32,16},{48,32},{64,48},{80,64},{96,80},{112,96},{128,112},... | collective-permute-start | bytes 786440 | tf_op jit(solution)/shard_map/while/body/eval_jaxpr/ppermute | solution.py:14
  116.2 7.7 %collective-permute-start = (bf16[8,64,256]{2,1,0:T(8,128)(2,1)S(1)}, bf16[8,64,256]{2,1,0:T(8,128)(2,1)S(1)}, u32[]{:S(2)}, u32[]{:S(2)}) collective-permute-start(bf16[8,64,256]{2,1,0:T(8,128)(2,1)S(1)} %add_convert_fusion.2), channel_id=1, source_target_pairs={{16,0},{32,16},{48,32},{64,48},{80,64},{96,80},{112,96},{128,112},... | collective-permute-start | bytes 786440 | tf_op jit(solution)/shard_map/while/body/eval_jaxpr/ppermute | solution.py:14
  124.0 7.7 %collective-permute-start = (bf16[8,64,256]{2,1,0:T(8,128)(2,1)S(1)}, bf16[8,64,256]{2,1,0:T(8,128)(2,1)S(1)}, u32[]{:S(2)}, u32[]{:S(2)}) collective-permute-start(bf16[8,64,256]{2,1,0:T(8,128)(2,1)S(1)} %add_convert_fusion.2), channel_id=1, source_target_pairs={{16,0},{32,16},{48,32},{64,48},{80,64},{96,80},{112,96},{128,112},... | collective-permute-start | bytes 786440 | tf_op jit(solution)/shard_map/while/body/eval_jaxpr/ppermute | solution.py:14
  131.9 7.7 %collective-permute-start = (bf16[8,64,256]{2,1,0:T(8,128)(2,1)S(1)}, bf16[8,64,256]{2,1,0:T(8,128)(2,1)S(1)}, u32[]{:S(2)}, u32[]{:S(2)}) collective-permute-start(bf16[8,64,256]{2,1,0:T(8,128)(2,1)S(1)} %add_convert_fusion.2), channel_id=1, source_target_pairs={{16,0},{32,16},{48,32},{64,48},{80,64},{96,80},{112,96},{128,112},... | collective-permute-start | bytes 786440 | tf_op jit(solution)/shard_map/while/body/eval_jaxpr/ppermute | solution.py:14
  139.7 5.7 %copy-start.2 = (f32[4,512]{1,0:T(4,128)S(1)}, f32[4,512]{1,0:T(4,128)}, u32[]{:S(2)}) copy-start(f32[4,512]{1,0:T(4,128)} %param.19) | copy-start | bytes 24580
  143.5 4.9 %collective-permute-start.1 = (bf16[3,512]{1,0:T(4,128)(2,1)S(1)}, bf16[3,512]{1,0:T(4,128)(2,1)S(1)}, u32[]{:S(2)}, u32[]{:S(2)}) collective-permute-start(bf16[3,512]{1,0:T(4,128)(2,1)S(1)} %slice.50), channel_id=1, source_target_pairs={{16,0},{32,16},{48,32},{64,48},{80,64},{96,80},{112,96},{128,112},... | collective-permute-start | bytes 9224 | tf_op jit(solution)/shard_map/ppermute | solution.py:14
  149.8 95.2 %reduce-scatter.2.cloned.1.call-start = ((), (), s32[]{:S(2)}) async-start(), calls=%async_computation.2 | async-start | bytes 2621440 | tf_op jit(solution)/shard_map/reduce_scatter | solution.py:89
Sparse Core Ops, SparseCore 0:
  150.0 52.5 all-gather.1
  212.6 32.3 reduce-scatter.1
where the time goes:
time: 253 us; the launch traced here: 252 us
  waiting for transfers between devices  172 us (68%)
  starting transfers between devices  34 us (13%)
  matrix products  17.7 us (7%)
  between operations  14.2 us (6%)
  other arithmetic  8.98 us (4%)
  local copies, waits for them, and re-layouts  4.6 us (2%)
    ppermute x16, waiting for transfers between devices, from_behind(): lax.ppermute(value, axis, [(source, source + steps) for source in range(f...  87.5 us
    all_gather x1, waiting for transfers between devices, on_device(): lax.all_gather(x_grad, 'col', axis=1, tiled=True)  52.7 us
    ppermute x16, starting transfers between devices, from_behind(): lax.ppermute(value, axis, [(source, source + steps) for source in range(f...  34 us
    reduce_scatter x1, waiting for transfers between devices, on_device(): lax.psum_scatter(partial_grad.astype(jnp.bfloat16), 'row', scatter_dimens...  31.6 us
    dot_general x1, matrix products, on_device(): lax.dot_general(lax.all_gather(x_grad, 'col', axis=1, tiled=True), proj_w...  9.85 us
  transfers between devices with their start and end apart: 18, of which 18 were waited for; matrix products, arithmetic and copies ran while one was open for 0% of the time, Pallas kernels for 0%

commit v1 on v0

--- a/solution.py
+++ b/solution.py
@@ -6,6 +6,12 @@
 HD = 64
 HPG = 32
 KW = 4
+
+
+def chains_arrange(shard_in, chip_axis):
+    ready = tuple((shard_in for _ in range(lax.psum(1, chip_axis))))
+    current_arr = jnp.concatenate(ready, 1)
+    return lax.all_to_all(current_arr, chip_axis, 1, 1, tiled=True)
 
 
 def from_behind(value, axis, steps):
@@ -81,7 +87,7 @@
         accum = accum + conv_weight[tap][None, :] * extended[tap : tap + tokens_dev]
     x_grad = accum.astype(jnp.bfloat16)
     partial_grad = lax.dot_general(
-        lax.all_gather(x_grad, "col", axis=1, tiled=True),
+        chains_arrange(x_grad, "col"),
         proj_weight,
         (((1,), (1,)), ((), ())),
         preferred_element_type=jnp.float32,

time: 253 us -> 253 us (level)
  waiting for transfers between devices: 172 us -> 136 us
  blocking collectives: 0 us -> 28.3 us
  local copies, waits for them, and re-layouts: 4.6 us -> 12.9 us
    all_gather x1 -> x0, waiting for transfers between devices: 52.7 us -> none  [on_device(): lax.all_gather(x_grad, 'col', axis=1, tiled=True)]
    all_to_all x0 -> x1, blocking collectives: none -> 28.3 us  [chains_arrange(): return lax.all_to_all(current_arr, chip_axis, 1, 1, tiled=True)]
    reduce_scatter x1, waiting for transfers between devices: 31.6 us -> 46.7 us  [on_device(): lax.psum_scatter(partial_grad.astype(jnp.bfloat16), 'row', scatter_dimens...]
    all_to_all x0 -> x2, local copies, waits for them, and re-layouts: none -> 4.77 us  [chains_arrange(): return lax.all_to_all(current_arr, chip_axis, 1, 1, tiled=True)]
    unnamed x9 -> x15, local copies, waits for them, and re-layouts: 1.27 us -> 5.17 us
  transfers between devices with their start and end apart: 18 -> 17, of which waited for: 18 -> 17; matrix products, arithmetic and copies ran while one was open for 0% -> 1% of each run, Pallas kernels for 0% -> 0%
where the time goes in v1:
time: 253 us; the launch traced here: 252 us
  waiting for transfers between devices  136 us (54%)
  starting transfers between devices  34 us (13%)
  blocking collectives  28.3 us (11%)
  matrix products  17.8 us (7%)
  between operations  14.2 us (6%)
  local copies, waits for them, and re-layouts  12.9 us (5%)
  other arithmetic  9.07 us (4%)
    ppermute x16, waiting for transfers between devices, from_behind(): lax.ppermute(value, axis, [(source, source + steps) for source in range(f...  88.8 us
    reduce_scatter x1, waiting for transfers between devices, on_device(): lax.psum_scatter(partial_grad.astype(jnp.bfloat16), 'row', scatter_dimens...  46.7 us
    ppermute x16, starting transfers between devices, from_behind(): lax.ppermute(value, axis, [(source, source + steps) for source in range(f...  34 us
    all_to_all x1, blocking collectives, chains_arrange(): return lax.all_to_all(current_arr, chip_axis, 1, 1, tiled=True)  28.3 us
    dot_general x1, matrix products, on_device(): lax.dot_general(chains_arrange(x_grad, 'col'), proj_weight, (((1,), (1,))...  9.93 us
    unnamed x15, local copies, waits for them, and re-layouts  5.17 us
  transfers between devices with their start and end apart: 17, of which 17 were waited for; matrix products, arithmetic and copies ran while one was open for 1% of the time, Pallas kernels for 0%

profile of v1, /device:TPU:1, one launch (start us, length us, event | category | flops | bytes accessed | tf_op | source)
XLA Modules:
  0.0 252.4 jit_solution(12940283608441111208)
XLA Ops:
  7.2 2.2 reduce-window.6
  9.4 0.2 slice_reduce_fusion
  9.7 0.2 slice_reduce_fusion.1
  10.1 1.3 copy.36
  11.4 2.0 copy.38
  13.6 2.6 %constant_dynamic-slice_fusion = (bf16[512,1,256]{2,1,0:T(2,128)(2,1)S(1)}, bf16[512,1,256]{2,1,0:T(2,128)(2,1)S(1)}) fusion(bf16[512,4,256]{2,1,0:T(4,128)(2,1)} %param.15, s32[]{:T(128)S(6)} %select_n.30, bf16[512,4,256]{2,1,0:T(4,128)(2,1)} %param.14), kind=kLoop, calls=%fused_computation.50 | loop fusion | bytes 1048580 | tf_op jit(solution)/shard_map/jit(dynamic_index_in_dim)/dynamic_slice | solution.py:40
  16.2 0.3 fusion.17
  16.5 1.4 fusion.20
  17.9 4.2 %fusion.2 = f32[512,8,64]{0,2,1:T(8,128)} fusion(bf16[512,8,64]{0,2,1:T(8,128)(2,1)S(1)} %bitcast.47, f32[512,512]{1,0:T(8,128)} %fusion.20, f32[8,512]{1,0:T(8,128)S(1)} %get-tuple-element.52, pred[512,512]{1,0:T(8,128)(4,1)S(1)} %iota_compare_fusion), kind=kOutput, calls=%fused_computation.7 | convolution fusion | flops 276824064 | bytes 2899968 | tf_op jit(solution)/shard_map/hts,shd->thd/dot_general | solution.py:71
  22.2 119.6 %while.10 = (s32[]{:T(128)}, f32[8,64,256]{2,1,0:T(8,128)S(1)}, pred[]{:T(512)}, f32[8]{0:T(128)S(1)}, f32[8,64,256]{2,1,0:T(8,128)S(1)}, /*index=5*/f32[8,64,256]{2,1,0:T(8,128)S(1)}, s32[]{:T(128)}) while((s32[]{:T(128)}, f32[8,64,256]{2,1,0:T(8,128)S(1)}, pred[]{:T(512)}, f32[8]{0:T(128)S(1)}, f32[8,64,256]{2,1,0:T(8,128)S(1)}, ...), condition=%wide.region_3.4_spmd, body=%wide.region_2.3_spmd.sunk | while | flops 655362 | bytes 3670166 | solution.py:57
  22.3 5.2 %collective-permute-start = (bf16[8,64,256]{2,1,0:T(8,128)(2,1)S(1)}, bf16[8,64,256]{2,1,0:T(8,128)(2,1)S(1)}, u32[]{:S(2)}, u32[]{:S(2)}) collective-permute-start(bf16[8,64,256]{2,1,0:T(8,128)(2,1)S(1)} %add_convert_fusion.2), channel_id=1, source_target_pairs={{16,0},{32,16},{48,32},{64,48},{80,64},{96,80},{112,96},{128,112},... | collective-permute-start | bytes 786440 | tf_op jit(solution)/shard_map/while/body/eval_jaxpr/ppermute | solution.py:20
  27.4 3.8 %collective-permute-done = bf16[8,64,256]{2,1,0:T(8,128)(2,1)S(1)} collective-permute-done((bf16[8,64,256]{2,1,0:T(8,128)(2,1)S(1)}, bf16[8,64,256]{2,1,0:T(8,128)(2,1)S(1)}, u32[]{:S(2)}, u32[]{:S(2)}) %collective-permute-start) | collective-permute-done | bytes 262176 | tf_op jit(solution)/shard_map/while/body/eval_jaxpr/ppermute | solution.py:20
  31.3 0.1 add_convert_fusion.2
  31.5 1.9 collective-permute-start
  33.4 5.8 %collective-permute-done = bf16[8,64,256]{2,1,0:T(8,128)(2,1)S(1)} collective-permute-done((bf16[8,64,256]{2,1,0:T(8,128)(2,1)S(1)}, bf16[8,64,256]{2,1,0:T(8,128)(2,1)S(1)}, u32[]{:S(2)}, u32[]{:S(2)}) %collective-permute-start) | collective-permute-done | bytes 262176 | tf_op jit(solution)/shard_map/while/body/eval_jaxpr/ppermute | solution.py:20
  39.2 0.1 add_convert_fusion.2
  39.4 1.9 collective-permute-start
  41.3 5.8 %collective-permute-done = bf16[8,64,256]{2,1,0:T(8,128)(2,1)S(1)} collective-permute-done((bf16[8,64,256]{2,1,0:T(8,128)(2,1)S(1)}, bf16[8,64,256]{2,1,0:T(8,128)(2,1)S(1)}, u32[]{:S(2)}, u32[]{:S(2)}) %collective-permute-start) | collective-permute-done | bytes 262176 | tf_op jit(solution)/shard_map/while/body/eval_jaxpr/ppermute | solution.py:20
  47.1 0.1 add_convert_fusion.2
  47.2 1.9 collective-permute-start
  49.2 5.8 %collective-permute-done = bf16[8,64,256]{2,1,0:T(8,128)(2,1)S(1)} collective-permute-done((bf16[8,64,256]{2,1,0:T(8,128)(2,1)S(1)}, bf16[8,64,256]{2,1,0:T(8,128)(2,1)S(1)}, u32[]{:S(2)}, u32[]{:S(2)}) %collective-permute-start) | collective-permute-done | bytes 262176 | tf_op jit(solution)/shard_map/while/body/eval_jaxpr/ppermute | solution.py:20
  55.0 0.1 add_convert_fusion.2
  55.1 1.9 collective-permute-start
  57.1 5.8 %collective-permute-done = bf16[8,64,256]{2,1,0:T(8,128)(2,1)S(1)} collective-permute-done((bf16[8,64,256]{2,1,0:T(8,128)(2,1)S(1)}, bf16[8,64,256]{2,1,0:T(8,128)(2,1)S(1)}, u32[]{:S(2)}, u32[]{:S(2)}) %collective-permute-start) | collective-permute-done | bytes 262176 | tf_op jit(solution)/shard_map/while/body/eval_jaxpr/ppermute | solution.py:20
  62.9 0.1 add_convert_fusion.2
  63.0 1.9 collective-permute-start
  64.9 5.8 %collective-permute-done = bf16[8,64,256]{2,1,0:T(8,128)(2,1)S(1)} collective-permute-done((bf16[8,64,256]{2,1,0:T(8,128)(2,1)S(1)}, bf16[8,64,256]{2,1,0:T(8,128)(2,1)S(1)}, u32[]{:S(2)}, u32[]{:S(2)}) %collective-permute-start) | collective-permute-done | bytes 262176 | tf_op jit(solution)/shard_map/while/body/eval_jaxpr/ppermute | solution.py:20
  70.8 0.1 add_convert_fusion.2
  70.9 1.9 collective-permute-start
  72.8 5.8 %collective-permute-done = bf16[8,64,256]{2,1,0:T(8,128)(2,1)S(1)} collective-permute-done((bf16[8,64,256]{2,1,0:T(8,128)(2,1)S(1)}, bf16[8,64,256]{2,1,0:T(8,128)(2,1)S(1)}, u32[]{:S(2)}, u32[]{:S(2)}) %collective-permute-start) | collective-permute-done | bytes 262176 | tf_op jit(solution)/shard_map/while/body/eval_jaxpr/ppermute | solution.py:20
  78.7 0.1 add_convert_fusion.2
  78.8 1.9 collective-permute-start
  80.7 5.8 %collective-permute-done = bf16[8,64,256]{2,1,0:T(8,128)(2,1)S(1)} collective-permute-done((bf16[8,64,256]{2,1,0:T(8,128)(2,1)S(1)}, bf16[8,64,256]{2,1,0:T(8,128)(2,1)S(1)}, u32[]{:S(2)}, u32[]{:S(2)}) %collective-permute-start) | collective-permute-done | bytes 262176 | tf_op jit(solution)/shard_map/while/body/eval_jaxpr/ppermute | solution.py:20
  86.5 0.1 add_convert_fusion.2
  86.7 1.9 collective-permute-start
  88.6 5.8 %collective-permute-done = bf16[8,64,256]{2,1,0:T(8,128)(2,1)S(1)} collective-permute-done((bf16[8,64,256]{2,1,0:T(8,128)(2,1)S(1)}, bf16[8,64,256]{2,1,0:T(8,128)(2,1)S(1)}, u32[]{:S(2)}, u32[]{:S(2)}) %collective-permute-start) | collective-permute-done | bytes 262176 | tf_op jit(solution)/shard_map/while/body/eval_jaxpr/ppermute | solution.py:20
  94.4 0.1 add_convert_fusion.2
  94.6 1.9 collective-permute-start
  96.5 5.8 %collective-permute-done = bf16[8,64,256]{2,1,0:T(8,128)(2,1)S(1)} collective-permute-done((bf16[8,64,256]{2,1,0:T(8,128)(2,1)S(1)}, bf16[8,64,256]{2,1,0:T(8,128)(2,1)S(1)}, u32[]{:S(2)}, u32[]{:S(2)}) %collective-permute-start) | collective-permute-done | bytes 262176 | tf_op jit(solution)/shard_map/while/body/eval_jaxpr/ppermute | solution.py:20
  102.3 0.1 add_convert_fusion.2
  102.4 1.9 collective-permute-start
  104.4 5.8 %collective-permute-done = bf16[8,64,256]{2,1,0:T(8,128)(2,1)S(1)} collective-permute-done((bf16[8,64,256]{2,1,0:T(8,128)(2,1)S(1)}, bf16[8,64,256]{2,1,0:T(8,128)(2,1)S(1)}, u32[]{:S(2)}, u32[]{:S(2)}) %collective-permute-start) | collective-permute-done | bytes 262176 | tf_op jit(solution)/shard_map/while/body/eval_jaxpr/ppermute | solution.py:20
  110.3 1.9 collective-permute-start
  112.3 5.8 %collective-permute-done = bf16[8,64,256]{2,1,0:T(8,128)(2,1)S(1)} collective-permute-done((bf16[8,64,256]{2,1,0:T(8,128)(2,1)S(1)}, bf16[8,64,256]{2,1,0:T(8,128)(2,1)S(1)}, u32[]{:S(2)}, u32[]{:S(2)}) %collective-permute-start) | collective-permute-done | bytes 262176 | tf_op jit(solution)/shard_map/while/body/eval_jaxpr/ppermute | solution.py:20
  118.2 1.9 collective-permute-start
  120.1 5.8 %collective-permute-done = bf16[8,64,256]{2,1,0:T(8,128)(2,1)S(1)} collective-permute-done((bf16[8,64,256]{2,1,0:T(8,128)(2,1)S(1)}, bf16[8,64,256]{2,1,0:T(8,128)(2,1)S(1)}, u32[]{:S(2)}, u32[]{:S(2)}) %collective-permute-start) | collective-permute-done | bytes 262176 | tf_op jit(solution)/shard_map/while/body/eval_jaxpr/ppermute | solution.py:20
  126.1 1.9 collective-permute-start
  128.0 5.8 %collective-permute-done = bf16[8,64,256]{2,1,0:T(8,128)(2,1)S(1)} collective-permute-done((bf16[8,64,256]{2,1,0:T(8,128)(2,1)S(1)}, bf16[8,64,256]{2,1,0:T(8,128)(2,1)S(1)}, u32[]{:S(2)}, u32[]{:S(2)}) %collective-permute-start) | collective-permute-done | bytes 262176 | tf_op jit(solution)/shard_map/while/body/eval_jaxpr/ppermute | solution.py:20
  134.0 1.9 collective-permute-start
  135.9 5.8 %collective-permute-done = bf16[8,64,256]{2,1,0:T(8,128)(2,1)S(1)} collective-permute-done((bf16[8,64,256]{2,1,0:T(8,128)(2,1)S(1)}, bf16[8,64,256]{2,1,0:T(8,128)(2,1)S(1)}, u32[]{:S(2)}, u32[]{:S(2)}) %collective-permute-start) | collective-permute-done | bytes 262176 | tf_op jit(solution)/shard_map/while/body/eval_jaxpr/ppermute | solution.py:20
  141.8 2.0 fusion.5
  143.8 1.5 fusion.11
  145.3 1.9 collective-permute-start.1
  147.2 4.3 %collective-permute-done.1 = bf16[3,512]{0,1:T(8,128)(2,1)S(1)} collective-permute-done((bf16[3,512]{0,1:T(8,128)(2,1)S(1)}, bf16[3,512]{0,1:T(8,128)(2,1)S(1)}, u32[]{:S(2)}, u32[]{:S(2)}) %collective-permute-start.1) | collective-permute-done | bytes 3104 | tf_op jit(solution)/shard_map/ppermute | solution.py:20
  151.6 1.2 fusion.13
  152.9 0.8 copy-done.1
  153.7 0.2 pad_maximum_fusion
  153.9 2.4 copy.39
  156.3 28.3 %all_to_all.12 = bf16[512,4,512]{2,0,1:T(8,128)(2,1)S(1)} all-to-all(bf16[512,4,512]{2,0,1:T(8,128)(2,1)} %copy.39), channel_id=1, replica_groups=mesh['ctx'=16,'row'=4,'col'=4] {'col'}, dimensions={1} | all-to-all | bytes 4194304 | tf_op jit(solution)/shard_map/all_to_all | solution.py:14
  184.6 2.4 copy.40
  187.0 9.9 %convolution_convert_fusion = bf16[512,2048]{1,0:T(8,128)(2,1)} fusion(bf16[512,2048]{0,1:T(8,128)(2,1)} %bitcast.49, bf16[2048,2048]{1,0:T(8,128)(2,1)} %param.21), kind=kOutput, calls=%fused_computation.5 | convolution fusion | flops 4296015872 | bytes 12582912 | tf_op jit(solution)/shard_map/dot_general | solution.py:89
  196.9 0.9 add_bitcast_fusion
  197.8 1.0 copy.41
  198.8 46.7 %reduce-scatter.2.cloned.1.call-done = bf16[512,512]{1,0:T(8,128)(2,1)} async-done(((bf16[512,2048]{1,0:T(8,128)(2,1)}), bf16[512,512]{1,0:T(8,128)(2,1)}) %reduce-scatter.2.cloned.1.call-update) | async-done | bytes 524304 | tf_op jit(solution)/shard_map/reduce_scatter | solution.py:95
  (44 shorter events, 2.0 us)
Async XLA Ops:
  7.2 238.4 %reduce-scatter.2.cloned.1.call-start = ((), (), s32[]{:S(2)}) async-start(), calls=%async_computation.2 | async-start | bytes 2621440 | tf_op jit(solution)/shard_map/reduce_scatter | solution.py:95
  10.0 7.9 %copy-start = (f32[8,64,256]{2,1,0:T(8,128)S(1)}, f32[8,64,256]{2,1,0:T(8,128)}, u32[]{:S(2)}) copy-start(f32[8,64,256]{2,1,0:T(8,128)} %param.20) | copy-start | bytes 1572868
  22.2 119.6 %copy-start.3 = (f32[8,512]{1,0:T(8,128)S(1)}, f32[8,512]{1,0:T(8,128)}, u32[]{:S(2)}) copy-start(f32[8,512]{1,0:T(8,128)} %param.16) | copy-start | bytes 49156
  22.2 119.6 %copy-start.5 = (f32[8]{0:T(128)S(1)}, f32[8]{0:T(128)}, u32[]{:S(2)}) copy-start(f32[8]{0:T(128)} %param.18) | copy-start | bytes 100
  22.3 9.0 %collective-permute-start = (bf16[8,64,256]{2,1,0:T(8,128)(2,1)S(1)}, bf16[8,64,256]{2,1,0:T(8,128)(2,1)S(1)}, u32[]{:S(2)}, u32[]{:S(2)}) collective-permute-start(bf16[8,64,256]{2,1,0:T(8,128)(2,1)S(1)} %add_convert_fusion.2), channel_id=1, source_target_pairs={{16,0},{32,16},{48,32},{64,48},{80,64},{96,80},{112,96},{128,112},... | collective-permute-start | bytes 786440 | tf_op jit(solution)/shard_map/while/body/eval_jaxpr/ppermute | solution.py:20
  31.5 7.7 %collective-permute-start = (bf16[8,64,256]{2,1,0:T(8,128)(2,1)S(1)}, bf16[8,64,256]{2,1,0:T(8,128)(2,1)S(1)}, u32[]{:S(2)}, u32[]{:S(2)}) collective-permute-start(bf16[8,64,256]{2,1,0:T(8,128)(2,1)S(1)} %add_convert_fusion.2), channel_id=1, source_target_pairs={{16,0},{32,16},{48,32},{64,48},{80,64},{96,80},{112,96},{128,112},... | collective-permute-start | bytes 786440 | tf_op jit(solution)/shard_map/while/body/eval_jaxpr/ppermute | solution.py:20
  39.4 7.7 %collective-permute-start = (bf16[8,64,256]{2,1,0:T(8,128)(2,1)S(1)}, bf16[8,64,256]{2,1,0:T(8,128)(2,1)S(1)}, u32[]{:S(2)}, u32[]{:S(2)}) collective-permute-start(bf16[8,64,256]{2,1,0:T(8,128)(2,1)S(1)} %add_convert_fusion.2), channel_id=1, source_target_pairs={{16,0},{32,16},{48,32},{64,48},{80,64},{96,80},{112,96},{128,112},... | collective-permute-start | bytes 786440 | tf_op jit(solution)/shard_map/while/body/eval_jaxpr/ppermute | solution.py:20
  47.2 7.7 %collective-permute-start = (bf16[8,64,256]{2,1,0:T(8,128)(2,1)S(1)}, bf16[8,64,256]{2,1,0:T(8,128)(2,1)S(1)}, u32[]{:S(2)}, u32[]{:S(2)}) collective-permute-start(bf16[8,64,256]{2,1,0:T(8,128)(2,1)S(1)} %add_convert_fusion.2), channel_id=1, source_target_pairs={{16,0},{32,16},{48,32},{64,48},{80,64},{96,80},{112,96},{128,112},... | collective-permute-start | bytes 786440 | tf_op jit(solution)/shard_map/while/body/eval_jaxpr/ppermute | solution.py:20
  55.1 7.7 %collective-permute-start = (bf16[8,64,256]{2,1,0:T(8,128)(2,1)S(1)}, bf16[8,64,256]{2,1,0:T(8,128)(2,1)S(1)}, u32[]{:S(2)}, u32[]{:S(2)}) collective-permute-start(bf16[8,64,256]{2,1,0:T(8,128)(2,1)S(1)} %add_convert_fusion.2), channel_id=1, source_target_pairs={{16,0},{32,16},{48,32},{64,48},{80,64},{96,80},{112,96},{128,112},... | collective-permute-start | bytes 786440 | tf_op jit(solution)/shard_map/while/body/eval_jaxpr/ppermute | solution.py:20
  63.0 7.7 %collective-permute-start = (bf16[8,64,256]{2,1,0:T(8,128)(2,1)S(1)}, bf16[8,64,256]{2,1,0:T(8,128)(2,1)S(1)}, u32[]{:S(2)}, u32[]{:S(2)}) collective-permute-start(bf16[8,64,256]{2,1,0:T(8,128)(2,1)S(1)} %add_convert_fusion.2), channel_id=1, source_target_pairs={{16,0},{32,16},{48,32},{64,48},{80,64},{96,80},{112,96},{128,112},... | collective-permute-start | bytes 786440 | tf_op jit(solution)/shard_map/while/body/eval_jaxpr/ppermute | solution.py:20
  70.9 7.7 %collective-permute-start = (bf16[8,64,256]{2,1,0:T(8,128)(2,1)S(1)}, bf16[8,64,256]{2,1,0:T(8,128)(2,1)S(1)}, u32[]{:S(2)}, u32[]{:S(2)}) collective-permute-start(bf16[8,64,256]{2,1,0:T(8,128)(2,1)S(1)} %add_convert_fusion.2), channel_id=1, source_target_pairs={{16,0},{32,16},{48,32},{64,48},{80,64},{96,80},{112,96},{128,112},... | collective-permute-start | bytes 786440 | tf_op jit(solution)/shard_map/while/body/eval_jaxpr/ppermute | solution.py:20
  78.8 7.7 %collective-permute-start = (bf16[8,64,256]{2,1,0:T(8,128)(2,1)S(1)}, bf16[8,64,256]{2,1,0:T(8,128)(2,1)S(1)}, u32[]{:S(2)}, u32[]{:S(2)}) collective-permute-start(bf16[8,64,256]{2,1,0:T(8,128)(2,1)S(1)} %add_convert_fusion.2), channel_id=1, source_target_pairs={{16,0},{32,16},{48,32},{64,48},{80,64},{96,80},{112,96},{128,112},... | collective-permute-start | bytes 786440 | tf_op jit(solution)/shard_map/while/body/eval_jaxpr/ppermute | solution.py:20
  86.7 7.7 %collective-permute-start = (bf16[8,64,256]{2,1,0:T(8,128)(2,1)S(1)}, bf16[8,64,256]{2,1,0:T(8,128)(2,1)S(1)}, u32[]{:S(2)}, u32[]{:S(2)}) collective-permute-start(bf16[8,64,256]{2,1,0:T(8,128)(2,1)S(1)} %add_convert_fusion.2), channel_id=1, source_target_pairs={{16,0},{32,16},{48,32},{64,48},{80,64},{96,80},{112,96},{128,112},... | collective-permute-start | bytes 786440 | tf_op jit(solution)/shard_map/while/body/eval_jaxpr/ppermute | solution.py:20
  94.6 7.7 %collective-permute-start = (bf16[8,64,256]{2,1,0:T(8,128)(2,1)S(1)}, bf16[8,64,256]{2,1,0:T(8,128)(2,1)S(1)}, u32[]{:S(2)}, u32[]{:S(2)}) collective-permute-start(bf16[8,64,256]{2,1,0:T(8,128)(2,1)S(1)} %add_convert_fusion.2), channel_id=1, source_target_pairs={{16,0},{32,16},{48,32},{64,48},{80,64},{96,80},{112,96},{128,112},... | collective-permute-start | bytes 786440 | tf_op jit(solution)/shard_map/while/body/eval_jaxpr/ppermute | solution.py:20
  102.4 7.7 %collective-permute-start = (bf16[8,64,256]{2,1,0:T(8,128)(2,1)S(1)}, bf16[8,64,256]{2,1,0:T(8,128)(2,1)S(1)}, u32[]{:S(2)}, u32[]{:S(2)}) collective-permute-start(bf16[8,64,256]{2,1,0:T(8,128)(2,1)S(1)} %add_convert_fusion.2), channel_id=1, source_target_pairs={{16,0},{32,16},{48,32},{64,48},{80,64},{96,80},{112,96},{128,112},... | collective-permute-start | bytes 786440 | tf_op jit(solution)/shard_map/while/body/eval_jaxpr/ppermute | solution.py:20
  110.3 7.7 %collective-permute-start = (bf16[8,64,256]{2,1,0:T(8,128)(2,1)S(1)}, bf16[8,64,256]{2,1,0:T(8,128)(2,1)S(1)}, u32[]{:S(2)}, u32[]{:S(2)}) collective-permute-start(bf16[8,64,256]{2,1,0:T(8,128)(2,1)S(1)} %add_convert_fusion.2), channel_id=1, source_target_pairs={{16,0},{32,16},{48,32},{64,48},{80,64},{96,80},{112,96},{128,112},... | collective-permute-start | bytes 786440 | tf_op jit(solution)/shard_map/while/body/eval_jaxpr/ppermute | solution.py:20
  118.2 7.7 %collective-permute-start = (bf16[8,64,256]{2,1,0:T(8,128)(2,1)S(1)}, bf16[8,64,256]{2,1,0:T(8,128)(2,1)S(1)}, u32[]{:S(2)}, u32[]{:S(2)}) collective-permute-start(bf16[8,64,256]{2,1,0:T(8,128)(2,1)S(1)} %add_convert_fusion.2), channel_id=1, source_target_pairs={{16,0},{32,16},{48,32},{64,48},{80,64},{96,80},{112,96},{128,112},... | collective-permute-start | bytes 786440 | tf_op jit(solution)/shard_map/while/body/eval_jaxpr/ppermute | solution.py:20
  126.1 7.7 %collective-permute-start = (bf16[8,64,256]{2,1,0:T(8,128)(2,1)S(1)}, bf16[8,64,256]{2,1,0:T(8,128)(2,1)S(1)}, u32[]{:S(2)}, u32[]{:S(2)}) collective-permute-start(bf16[8,64,256]{2,1,0:T(8,128)(2,1)S(1)} %add_convert_fusion.2), channel_id=1, source_target_pairs={{16,0},{32,16},{48,32},{64,48},{80,64},{96,80},{112,96},{128,112},... | collective-permute-start | bytes 786440 | tf_op jit(solution)/shard_map/while/body/eval_jaxpr/ppermute | solution.py:20
  134.0 7.7 %collective-permute-start = (bf16[8,64,256]{2,1,0:T(8,128)(2,1)S(1)}, bf16[8,64,256]{2,1,0:T(8,128)(2,1)S(1)}, u32[]{:S(2)}, u32[]{:S(2)}) collective-permute-start(bf16[8,64,256]{2,1,0:T(8,128)(2,1)S(1)} %add_convert_fusion.2), channel_id=1, source_target_pairs={{16,0},{32,16},{48,32},{64,48},{80,64},{96,80},{112,96},{128,112},... | collective-permute-start | bytes 786440 | tf_op jit(solution)/shard_map/while/body/eval_jaxpr/ppermute | solution.py:20
  141.8 5.4 %copy-start.4 = (f32[4,512]{1,0:T(4,128)S(1)}, f32[4,512]{1,0:T(4,128)}, u32[]{:S(2)}) copy-start(f32[4,512]{1,0:T(4,128)} %param.19) | copy-start | bytes 24580
  145.3 6.3 %collective-permute-start.1 = (bf16[3,512]{0,1:T(8,128)(2,1)S(1)}, bf16[3,512]{0,1:T(8,128)(2,1)S(1)}, u32[]{:S(2)}, u32[]{:S(2)}) collective-permute-start(bf16[3,512]{0,1:T(8,128)(2,1)S(1)} %slice.50), channel_id=1, source_target_pairs={{16,0},{32,16},{48,32},{64,48},{80,64},{96,80},{112,96},{128,112},... | collective-permute-start | bytes 9224 | tf_op jit(solution)/shard_map/ppermute | solution.py:20
  152.9 0.8 copy-start.1
  187.0 10.9 %copy-start.2 = (bf16[512,512]{0,1:T(8,128)(2,1)S(1)}, bf16[512,512]{0,1:T(8,128)(2,1)}, u32[]{:S(2)}) copy-start(bf16[512,512]{0,1:T(8,128)(2,1)} %copy-done.1) | copy-start | bytes 1572868
Sparse Core Ops, SparseCore 0:
  197.0 48.4 reduce-scatter.1
